TPU v7x, 256 devices: a whole 4x4x8 slice. The times are simulated.
256 devices in a mesh: row: 16 (over z_hi, y), col: 16 (over z_lo, x, core).
Axes of the slice: x: 4, y: 4, z: 8 (z_hi: 4, z_lo: 2; z = z_hi * 2 + z_lo), core: 2. Of those that a mesh axis runs over, the one named last changes fastest.
Arguments:
- right_side: float32 [16, 16, 1024, 256], P('row', 'col'), may hold values from -4 to 4
- local_operator: bfloat16 [16, 16, 1536, 1536], P('row', 'col'), may hold values from -1 to 4
- local_inverse: bfloat16 [16, 16, 1536, 1536], P('row', 'col'), may hold values from -1 to 1
- coarse_basis: bfloat16 [16, 16, 1536, 32], P('row', 'col'), may hold values from -1 to 1
- coarse_inverse: bfloat16 [16, 512, 8192], P(None, 'col', 'row'), may hold values from -1 to 1
- send_rows: int32 [16, 16, 4, 128], P('row', 'col'), may hold values from 0 to 1023, as said below
- send_count: int32 [16, 16, 4], P('row', 'col'), may hold values from 0 to 128, as said below
Outputs:
- solution: float32 [16, 16, 1024, 256], P('row', 'col')
Inputs may be any that keep to these rules, and one draw needn't show every extreme that they name: `send_rows`: within one subdomain and direction the entries are distinct owned rows; entries at or past that direction's count are ignored. `send_count`: 0 exactly where the neighbour in that direction lies outside the grid of subdomains; otherwise from 128 // 4 to 128, and 128 is reached.
All inputs are finite; a program needn't handle non-finite values.
Results may differ from a plain program's by a relative error of at most 0.023.
Values may be sent and summed in bfloat16 or wider, within the bound.
A program may use at most 64 MiB of HBM per device.

v0:
```python
import jax
import jax.numpy as jnp
from jax import lax
from jax.sharding import PartitionSpec as P

ITERS = 3


DAMPING = 0.5


def passed_along(shard, axis, by):
    devices = lax.axis_size(axis)
    pairs = [(i, i + by) for i in range(devices) if 0 <= i + by < devices]
    return lax.ppermute(shard, axis, pairs)


def ghost_trade(buffer):
    arrived = []
    for offset, source in ((1, 1), (-1, 0)):
        arrived.append(passed_along(buffer[source], "row", offset))
    for offset, source in ((1, 3), (-1, 2)):
        arrived.append(passed_along(buffer[source], "col", offset))
    return jnp.stack(arrived)


def per_device(
    right_side, local_operator, local_inverse, coarse_basis, coarse_inverse, send_rows, send_count
):
    target = right_side[0, 0]
    operator = local_operator[0, 0]
    inverse = local_inverse[0, 0]
    prolong = coarse_basis[0, 0]
    rows_list = send_rows[0, 0]
    counts = send_count[0, 0]
    own_rows, columns = target.shape
    tile_rows = rows_list.shape[1]
    live_mask = (lax.broadcasted_iota(jnp.int32, rows_list.shape, 1) < counts[:, None]).astype(
        jnp.float32
    )
    live_half = live_mask[..., None].astype(jnp.bfloat16)
    flat_rows = rows_list.reshape(-1)
    coarse_rows = coarse_inverse.reshape(-1, coarse_inverse.shape[2])

    def with_ghosts(values_half):
        packed = values_half[flat_rows].reshape(4, tile_rows, columns) * live_half
        ghosts = ghost_trade(packed)
        return jnp.concatenate([values_half, ghosts.reshape(4 * tile_rows, columns)], axis=0)

    def owner_sum(local_terms):
        rim_half = local_terms[own_rows:].astype(jnp.bfloat16).reshape(4, tile_rows, columns)
        returned = ghost_trade(rim_half)
        weighted = returned.astype(jnp.float32) * live_mask[..., None]
        summed = (
            jnp.zeros((own_rows, columns), jnp.float32)
            .at[flat_rows]
            .add(weighted.reshape(-1, columns))
        )
        return local_terms[:own_rows] + summed

    solution = jnp.zeros((own_rows, columns), jnp.float32)
    for sweep in range(ITERS):
        if sweep == 0:
            residual_half = target.astype(jnp.bfloat16)
        else:
            solution_half = solution.astype(jnp.bfloat16)
            image = owner_sum(
                jnp.dot(operator, with_ghosts(solution_half), preferred_element_type=jnp.float32)
            )
            residual_half = (target - image).astype(jnp.bfloat16)
        residual_local = with_ghosts(residual_half)
        local_part = jnp.dot(inverse, residual_local, preferred_element_type=jnp.float32)
        restricted = lax.dot_general(
            prolong, residual_local, (((0,), (0,)), ((), ())), preferred_element_type=jnp.float32
        )
        restricted = restricted.astype(jnp.bfloat16)
        block_rows = lax.all_gather(restricted, "col", axis=0, tiled=True)
        solved = lax.psum_scatter(
            jnp.dot(coarse_rows, block_rows, preferred_element_type=jnp.float32).astype(
                jnp.bfloat16
            ),
            "row",
            scatter_dimension=0,
            tiled=True,
        )
        update = owner_sum(
            local_part + jnp.dot(prolong, solved, preferred_element_type=jnp.float32)
        )
        solution = solution + DAMPING * update
    return solution[None, None]


def solution(mesh):
    return jax.shard_map(
        per_device,
        mesh=mesh,
        in_specs=(
            P("row", "col", None, None),
            P("row", "col", None, None),
            P("row", "col", None, None),
            P("row", "col", None, None),
            P(None, "col", "row"),
            P("row", "col", None, None),
            P("row", "col", None),
        ),
        out_specs=P("row", "col", None, None),
        check_vma=False,
    )
```

profile of v0, /device:TPU:1, one launch (start us, length us, event | category | flops | bytes accessed | tf_op | source)
XLA Modules:
  0.0 577.5 jit_solution(5471875140377850859)
XLA Ops:
  11.4 4.0 collective-permute-start
  22.7 4.4 collective-permute-done.1
  27.4 20.4 %all_gather.9 = bf16[512,256]{1,0:T(8,128)(2,1)S(1)} all-gather(bf16[32,256]{1,0:T(8,128)(2,1)S(1)} %fusion.22), channel_id=1, replica_groups=mesh['row'=16,'col'=16] {'col'}, dimensions={0}, use_global_device_ids=true | all-gather | bytes 278528 | tf_op jit(solution)/shard_map/all_gather | solution.py:77
  52.8 84.1 %reduce-scatter.10.cloned.1.call-done = bf16[32,256]{1,0:T(8,128)(2,1)} async-done(((bf16[512,256]{1,0:T(8,128)(2,1)}), bf16[32,256]{1,0:T(8,128)(2,1)}) %reduce-scatter.10.cloned.1.call-update) | async-done | bytes 16400
  140.1 5.2 collective-permute-start.7
  150.1 4.1 collective-permute-done.5
  170.5 4.3 collective-permute-done.9
  178.7 7.2 %collective-permute-start.12 = (bf16[128,256]{0,1:T(8,128)(2,1)S(1)}, bf16[128,256]{0,1:T(8,128)(2,1)S(1)}, u32[]{:S(2)}, u32[]{:S(2)}) collective-permute-start(bf16[128,256]{0,1:T(8,128)(2,1)S(1)} %get-tuple-element.17), channel_id=1, source_target_pairs={{0,16},{16,32},{32,48},{48,64},{64,80},{80,96},{96,112},{112,128},... | collective-permute-start | bytes 196616 | tf_op jit(solution)/shard_map/ppermute | solution.py:15
  206.9 4.5 collective-permute-start.16
  218.4 4.2 collective-permute-done.17
  222.9 18.3 %all_gather.10 = bf16[512,256]{1,0:T(8,128)(2,1)S(1)} all-gather(bf16[32,256]{1,0:T(8,128)(2,1)S(1)} %fusion.23), channel_id=1, replica_groups=mesh['row'=16,'col'=16] {'col'}, dimensions={0}, use_global_device_ids=true | all-gather | bytes 278528 | tf_op jit(solution)/shard_map/all_gather | solution.py:77
  242.5 5.0 fusion.6
  247.5 89.7 %reduce-scatter.12.cloned.1.call-done = bf16[32,256]{1,0:T(8,128)(2,1)} async-done(((bf16[512,256]{1,0:T(8,128)(2,1)}), bf16[32,256]{1,0:T(8,128)(2,1)}) %reduce-scatter.12.cloned.1.call-update) | async-done | bytes 16400
  341.1 5.1 collective-permute-start.23
  373.3 4.3 collective-permute-done.25
  381.5 7.5 %collective-permute-start.28 = (bf16[128,256]{0,1:T(8,128)(2,1)S(1)}, bf16[128,256]{0,1:T(8,128)(2,1)S(1)}, u32[]{:S(2)}, u32[]{:S(2)}) collective-permute-start(bf16[128,256]{0,1:T(8,128)(2,1)S(1)} %get-tuple-element.9), channel_id=1, source_target_pairs={{0,16},{16,32},{32,48},{48,64},{64,80},{80,96},{96,112},{112,128},... | collective-permute-start | bytes 196616 | tf_op jit(solution)/shard_map/ppermute | solution.py:15
  402.7 5.2 scatter_fusion.3
  411.7 4.4 collective-permute-start.32
  423.1 4.2 collective-permute-done.33
  428.1 18.4 %all_gather.11 = bf16[512,256]{1,0:T(8,128)(2,1)S(1)} all-gather(bf16[32,256]{1,0:T(8,128)(2,1)S(1)} %fusion.24), channel_id=1, replica_groups=mesh['row'=16,'col'=16] {'col'}, dimensions={0}, use_global_device_ids=true | all-gather | bytes 278528 | tf_op jit(solution)/shard_map/all_gather | solution.py:77
  447.7 5.0 fusion.4
  452.8 90.6 %reduce-scatter.14.cloned.1.call-done = bf16[32,256]{1,0:T(8,128)(2,1)} async-done(((bf16[512,256]{1,0:T(8,128)(2,1)}), bf16[32,256]{1,0:T(8,128)(2,1)}) %reduce-scatter.14.cloned.1.call-update) | async-done | bytes 16400
  547.2 5.1 collective-permute-start.39
  563.4 5.2 scatter_fusion.4
  (155 shorter events, 152.9 us)
Async XLA Ops:
  6.5 130.4 %reduce-scatter.10.cloned.1.call-start = ((), (), s32[]{:S(2)}) async-start(), calls=%async_computation.3 | async-start | bytes 278528
  11.4 11.2 %collective-permute-start = (bf16[128,256]{1,0:T(8,128)(2,1)S(1)}, bf16[128,256]{1,0:T(8,128)(2,1)S(1)}, u32[]{:S(2)}, u32[]{:S(2)}) collective-permute-start(bf16[128,256]{1,0:T(8,128)(2,1)S(1)} %get-tuple-element.41), channel_id=1, source_target_pairs={{0,16},{16,32},{32,48},{48,64},{64,80},{80,96},{96,112},{112,128},... | collective-permute-start | bytes 196616 | tf_op jit(solution)/shard_map/ppermute | solution.py:15
  15.5 7.2 %collective-permute-start.3 = (bf16[128,256]{1,0:T(8,128)(2,1)S(1)}, bf16[128,256]{1,0:T(8,128)(2,1)S(1)}, u32[]{:S(2)}, u32[]{:S(2)}) collective-permute-start(bf16[128,256]{1,0:T(8,128)(2,1)S(1)} %get-tuple-element.42), channel_id=1, source_target_pairs={{1,0},{2,1},{3,2},{4,3},{5,4},{6,5},{7,6},{8,7},{9,8},{10,9},{11,1... | collective-permute-start | bytes 196616 | tf_op jit(solution)/shard_map/ppermute | solution.py:15
  49.0 288.2 %reduce-scatter.12.cloned.1.call-start = ((), (), s32[]{:S(2)}) async-start(), calls=%async_computation.4 | async-start | bytes 278528
  138.1 11.9 %collective-permute-start.4 = (bf16[128,256]{0,1:T(8,128)(2,1)S(1)}, bf16[128,256]{0,1:T(8,128)(2,1)S(1)}, u32[]{:S(2)}, u32[]{:S(2)}) collective-permute-start(bf16[128,256]{0,1:T(8,128)(2,1)S(1)} %get-tuple-element.21), channel_id=1, source_target_pairs={{0,16},{16,32},{32,48},{48,64},{64,80},{80,96},{96,112},{112,128},... | collective-permute-start | bytes 196616 | tf_op jit(solution)/shard_map/ppermute | solution.py:15
  140.1 9.9 %collective-permute-start.7 = (bf16[128,256]{0,1:T(8,128)(2,1)S(1)}, bf16[128,256]{0,1:T(8,128)(2,1)S(1)}, u32[]{:S(2)}, u32[]{:S(2)}) collective-permute-start(bf16[128,256]{0,1:T(8,128)(2,1)S(1)} %get-tuple-element.22), channel_id=1, source_target_pairs={{1,0},{2,1},{3,2},{4,3},{5,4},{6,5},{7,6},{8,7},{9,8},{10,9},{11,1... | collective-permute-start | bytes 196616 | tf_op jit(solution)/shard_map/ppermute | solution.py:15
  160.5 10.0 %collective-permute-start.8 = (bf16[128,256]{1,0:T(8,128)(2,1)S(1)}, bf16[128,256]{1,0:T(8,128)(2,1)S(1)}, u32[]{:S(2)}, u32[]{:S(2)}) collective-permute-start(bf16[128,256]{1,0:T(8,128)(2,1)S(1)} %get-tuple-element.37), channel_id=1, source_target_pairs={{0,16},{16,32},{32,48},{48,64},{64,80},{80,96},{96,112},{112,128},... | collective-permute-start | bytes 196616 | tf_op jit(solution)/shard_map/ppermute | solution.py:15
  178.7 16.8 %collective-permute-start.12 = (bf16[128,256]{0,1:T(8,128)(2,1)S(1)}, bf16[128,256]{0,1:T(8,128)(2,1)S(1)}, u32[]{:S(2)}, u32[]{:S(2)}) collective-permute-start(bf16[128,256]{0,1:T(8,128)(2,1)S(1)} %get-tuple-element.17), channel_id=1, source_target_pairs={{0,16},{16,32},{32,48},{48,64},{64,80},{80,96},{96,112},{112,128},... | collective-permute-start | bytes 196616 | tf_op jit(solution)/shard_map/ppermute | solution.py:15
  185.9 9.5 %collective-permute-start.15 = (bf16[128,256]{0,1:T(8,128)(2,1)S(1)}, bf16[128,256]{0,1:T(8,128)(2,1)S(1)}, u32[]{:S(2)}, u32[]{:S(2)}) collective-permute-start(bf16[128,256]{0,1:T(8,128)(2,1)S(1)} %get-tuple-element.18), channel_id=1, source_target_pairs={{1,0},{2,1},{3,2},{4,3},{5,4},{6,5},{7,6},{8,7},{9,8},{10,9},{11,1... | collective-permute-start | bytes 196616 | tf_op jit(solution)/shard_map/ppermute | solution.py:15
  188.4 7.0 %collective-permute-start.14 = (bf16[128,256]{0,1:T(8,128)(2,1)S(1)}, bf16[128,256]{0,1:T(8,128)(2,1)S(1)}, u32[]{:S(2)}, u32[]{:S(2)}) collective-permute-start(bf16[128,256]{0,1:T(8,128)(2,1)S(1)} %get-tuple-element.19), channel_id=1, source_target_pairs={{0,1},{1,2},{2,3},{3,4},{4,5},{5,6},{6,7},{7,8},{8,9},{9,10},{10,1... | collective-permute-start | bytes 196616 | tf_op jit(solution)/shard_map/ppermute | solution.py:15
  206.9 11.4 %collective-permute-start.16 = (bf16[128,256]{1,0:T(8,128)(2,1)S(1)}, bf16[128,256]{1,0:T(8,128)(2,1)S(1)}, u32[]{:S(2)}, u32[]{:S(2)}) collective-permute-start(bf16[128,256]{1,0:T(8,128)(2,1)S(1)} %get-tuple-element.33), channel_id=1, source_target_pairs={{0,16},{16,32},{32,48},{48,64},{64,80},{80,96},{96,112},{112,128},... | collective-permute-start | bytes 196616 | tf_op jit(solution)/shard_map/ppermute | solution.py:15
  211.4 7.0 %collective-permute-start.19 = (bf16[128,256]{1,0:T(8,128)(2,1)S(1)}, bf16[128,256]{1,0:T(8,128)(2,1)S(1)}, u32[]{:S(2)}, u32[]{:S(2)}) collective-permute-start(bf16[128,256]{1,0:T(8,128)(2,1)S(1)} %get-tuple-element.34), channel_id=1, source_target_pairs={{1,0},{2,1},{3,2},{4,3},{5,4},{6,5},{7,6},{8,7},{9,8},{10,9},{11,1... | collective-permute-start | bytes 196616 | tf_op jit(solution)/shard_map/ppermute | solution.py:15
  242.5 300.9 %reduce-scatter.14.cloned.1.call-start = ((), (), s32[]{:S(2)}) async-start(), calls=%async_computation.5 | async-start | bytes 278528
  339.1 14.1 %collective-permute-start.20 = (bf16[128,256]{0,1:T(8,128)(2,1)S(1)}, bf16[128,256]{0,1:T(8,128)(2,1)S(1)}, u32[]{:S(2)}, u32[]{:S(2)}) collective-permute-start(bf16[128,256]{0,1:T(8,128)(2,1)S(1)} %get-tuple-element.13), channel_id=1, source_target_pairs={{0,16},{16,32},{32,48},{48,64},{64,80},{80,96},{96,112},{112,128},... | collective-permute-start | bytes 196616 | tf_op jit(solution)/shard_map/ppermute | solution.py:15
  341.1 12.1 %collective-permute-start.23 = (bf16[128,256]{0,1:T(8,128)(2,1)S(1)}, bf16[128,256]{0,1:T(8,128)(2,1)S(1)}, u32[]{:S(2)}, u32[]{:S(2)}) collective-permute-start(bf16[128,256]{0,1:T(8,128)(2,1)S(1)} %get-tuple-element.14), channel_id=1, source_target_pairs={{1,0},{2,1},{3,2},{4,3},{5,4},{6,5},{7,6},{8,7},{9,8},{10,9},{11,1... | collective-permute-start | bytes 196616 | tf_op jit(solution)/shard_map/ppermute | solution.py:15
  363.2 10.1 %collective-permute-start.24 = (bf16[128,256]{1,0:T(8,128)(2,1)S(1)}, bf16[128,256]{1,0:T(8,128)(2,1)S(1)}, u32[]{:S(2)}, u32[]{:S(2)}) collective-permute-start(bf16[128,256]{1,0:T(8,128)(2,1)S(1)} %get-tuple-element.29), channel_id=1, source_target_pairs={{0,16},{16,32},{32,48},{48,64},{64,80},{80,96},{96,112},{112,128},... | collective-permute-start | bytes 196616 | tf_op jit(solution)/shard_map/ppermute | solution.py:15
  381.5 18.0 %collective-permute-start.28 = (bf16[128,256]{0,1:T(8,128)(2,1)S(1)}, bf16[128,256]{0,1:T(8,128)(2,1)S(1)}, u32[]{:S(2)}, u32[]{:S(2)}) collective-permute-start(bf16[128,256]{0,1:T(8,128)(2,1)S(1)} %get-tuple-element.9), channel_id=1, source_target_pairs={{0,16},{16,32},{32,48},{48,64},{64,80},{80,96},{96,112},{112,128},... | collective-permute-start | bytes 196616 | tf_op jit(solution)/shard_map/ppermute | solution.py:15
  389.1 10.5 %collective-permute-start.31 = (bf16[128,256]{0,1:T(8,128)(2,1)S(1)}, bf16[128,256]{0,1:T(8,128)(2,1)S(1)}, u32[]{:S(2)}, u32[]{:S(2)}) collective-permute-start(bf16[128,256]{0,1:T(8,128)(2,1)S(1)} %get-tuple-element.10), channel_id=1, source_target_pairs={{1,0},{2,1},{3,2},{4,3},{5,4},{6,5},{7,6},{8,7},{9,8},{10,9},{11,1... | collective-permute-start | bytes 196616 | tf_op jit(solution)/shard_map/ppermute | solution.py:15
  391.6 8.0 %collective-permute-start.30 = (bf16[128,256]{0,1:T(8,128)(2,1)S(1)}, bf16[128,256]{0,1:T(8,128)(2,1)S(1)}, u32[]{:S(2)}, u32[]{:S(2)}) collective-permute-start(bf16[128,256]{0,1:T(8,128)(2,1)S(1)} %get-tuple-element.11), channel_id=1, source_target_pairs={{0,1},{1,2},{2,3},{3,4},{4,5},{5,6},{6,7},{7,8},{8,9},{9,10},{10,1... | collective-permute-start | bytes 196616 | tf_op jit(solution)/shard_map/ppermute | solution.py:15
  411.7 11.4 %collective-permute-start.32 = (bf16[128,256]{1,0:T(8,128)(2,1)S(1)}, bf16[128,256]{1,0:T(8,128)(2,1)S(1)}, u32[]{:S(2)}, u32[]{:S(2)}) collective-permute-start(bf16[128,256]{1,0:T(8,128)(2,1)S(1)} %get-tuple-element.25), channel_id=1, source_target_pairs={{0,16},{16,32},{32,48},{48,64},{64,80},{80,96},{96,112},{112,128},... | collective-permute-start | bytes 196616 | tf_op jit(solution)/shard_map/ppermute | solution.py:15
  416.1 7.0 %collective-permute-start.35 = (bf16[128,256]{1,0:T(8,128)(2,1)S(1)}, bf16[128,256]{1,0:T(8,128)(2,1)S(1)}, u32[]{:S(2)}, u32[]{:S(2)}) collective-permute-start(bf16[128,256]{1,0:T(8,128)(2,1)S(1)} %get-tuple-element.26), channel_id=1, source_target_pairs={{1,0},{2,1},{3,2},{4,3},{5,4},{6,5},{7,6},{8,7},{9,8},{10,9},{11,1... | collective-permute-start | bytes 196616 | tf_op jit(solution)/shard_map/ppermute | solution.py:15
  545.2 15.1 %collective-permute-start.36 = (bf16[128,256]{0,1:T(8,128)(2,1)S(1)}, bf16[128,256]{0,1:T(8,128)(2,1)S(1)}, u32[]{:S(2)}, u32[]{:S(2)}) collective-permute-start(bf16[128,256]{0,1:T(8,128)(2,1)S(1)} %get-tuple-element.5), channel_id=1, source_target_pairs={{0,16},{16,32},{32,48},{48,64},{64,80},{80,96},{96,112},{112,128},... | collective-permute-start | bytes 196616 | tf_op jit(solution)/shard_map/ppermute | solution.py:15
  547.2 13.1 %collective-permute-start.39 = (bf16[128,256]{0,1:T(8,128)(2,1)S(1)}, bf16[128,256]{0,1:T(8,128)(2,1)S(1)}, u32[]{:S(2)}, u32[]{:S(2)}) collective-permute-start(bf16[128,256]{0,1:T(8,128)(2,1)S(1)} %get-tuple-element.6), channel_id=1, source_target_pairs={{1,0},{2,1},{3,2},{4,3},{5,4},{6,5},{7,6},{8,7},{9,8},{10,9},{11,1... | collective-permute-start | bytes 196616 | tf_op jit(solution)/shard_map/ppermute | solution.py:15
  552.4 7.9 %collective-permute-start.38 = (bf16[128,256]{0,1:T(8,128)(2,1)S(1)}, bf16[128,256]{0,1:T(8,128)(2,1)S(1)}, u32[]{:S(2)}, u32[]{:S(2)}) collective-permute-start(bf16[128,256]{0,1:T(8,128)(2,1)S(1)} %get-tuple-element.7), channel_id=1, source_target_pairs={{0,1},{1,2},{2,3},{3,4},{4,5},{5,6},{6,7},{7,8},{8,9},{9,10},{10,1... | collective-permute-start | bytes 196616 | tf_op jit(solution)/shard_map/ppermute | solution.py:15
  (22 other events, 165.4 us)
Sparse Core Ops, SparseCore 0:
  49.1 87.7 reduce-scatter.9
  242.6 94.5 reduce-scatter.11
  447.8 95.4 reduce-scatter.13
where the time goes:
time: 584 us; the launch traced here: 578 us
  waiting for transfers between devices  295 us (51%)
  starting transfers between devices  117 us (20%)
  blocking collectives  57.1 us (10%)
  other arithmetic  36 us (6%)
  local copies, waits for them, and re-layouts  30.1 us (5%)
  matrix products  27.8 us (5%)
  between operations  14.1 us (2%)
    unnamed x6, waiting for transfers between devices  264 us
    ppermute x40, starting transfers between devices, passed_along(): return lax.ppermute(shard, axis, pairs)  117 us
    all_gather x3, blocking collectives, per_device(): block_rows = lax.all_gather(restricted, 'col', axis=0, tiled=True)  57.1 us
    ppermute x40, waiting for transfers between devices, passed_along(): return lax.ppermute(shard, axis, pairs)  31 us
    scatter-add x5, other arithmetic, owner_sum(): summed = jnp.zeros((own_rows, columns), jnp.float32).at[flat_rows].add(we...  21.8 us
    dot_general x3, matrix products, per_device(): jnp.dot(inverse, residual_local, preferred_element_type=jnp.float32)  13.8 us
    slice x10, local copies, waits for them, and re-layouts, owner_sum(): return local_terms[:own_rows] + summed  12.9 us
  transfers between devices with their start and end apart: 43, of which 13 were waited for; matrix products, arithmetic and copies ran while one was open for 5% of the time, Pallas kernels for 0%

commit v1 on v0

v1 whole, which is shorter than its diff:
```python
import functools

import jax
import jax.numpy as jnp
from jax import lax
from jax.experimental import pallas as pl
from jax.experimental.pallas import tpu as pltpu
from jax.sharding import PartitionSpec as P

ITERS = 3
DAMPING = 0.5
MESH = pl.DeviceIdType.MESH
OPPOSITE = (1, 0, 3, 2)
F32 = jnp.float32
HALF = jnp.bfloat16


def dot(left, right):
    return jnp.dot(left, right, preferred_element_type=F32)


def kernel(
    n_row, n_col,
    target_hbm, operator_hbm, inverse_hbm, basis_ref, coarse_hbm, rows_ref, counts_ref,
    out_ref,
    operator, inverse, coarse, target, basis_turned, pick, spread, total, values, held,
    packed, ghosts, gather_src, gathered, part_src, parts,
    load_sem, pack_send, pack_recv, gather_send, gather_recv, part_send, part_recv,
):
    own, width = target.shape
    tiles, tile = rows_ref.shape
    rim = tiles * tile
    level = basis_ref.shape[1]
    row = lax.axis_index("row")
    col = lax.axis_index("col")

    def at_row(step):
        return (lax.rem(row + step, n_row), col)

    def at_col(step):
        return (row, lax.rem(col + step, n_col))

    neighbours = (at_row(n_row - 1), at_row(1), at_col(n_col - 1), at_col(1))

    loads = [
        pltpu.make_async_copy(source, place, load_sem.at[i])
        for i, (source, place) in enumerate(
            (
                (target_hbm, target),
                (inverse_hbm, inverse),
                (coarse_hbm, coarse),
                (operator_hbm, operator),
            )
        )
    ]
    for load in loads:
        load.start()

    barrier = pltpu.get_barrier_semaphore()

    def greet_row(i, carry):
        pl.semaphore_signal(barrier, inc=1, device_id=at_row(i + 1), device_id_type=MESH)
        return carry

    def greet_col(i, carry):
        pl.semaphore_signal(barrier, inc=1, device_id=at_col(i + 1), device_id_type=MESH)
        return carry

    lax.fori_loop(0, n_row - 1, greet_row, 0)
    lax.fori_loop(0, n_col - 1, greet_col, 0)

    place = lax.broadcasted_iota(jnp.int32, (1, tile), 1)
    square = lax.broadcasted_iota(jnp.int32, (tile, tile), 0) == lax.broadcasted_iota(
        jnp.int32, (tile, tile), 1
    )
    for d in range(tiles):
        listed = jnp.where(place < counts_ref[0, d], rows_ref[d : d + 1, :], -1).astype(F32)
        down = lax.broadcasted_iota(jnp.int32, (own, tile), 0).astype(F32)
        spread[:, d * tile : (d + 1) * tile] = jnp.where(down == listed, 1.0, 0.0).astype(HALF)
        upright = jnp.sum(
            jnp.where(square, jnp.broadcast_to(listed, (tile, tile)), 0.0), axis=1, keepdims=True
        )
        along = lax.broadcasted_iota(jnp.int32, (tile, own), 1).astype(F32)
        pick[d * tile : (d + 1) * tile, :] = jnp.where(along == upright, 1.0, 0.0).astype(HALF)
    basis_turned[...] = basis_ref[...].astype(F32).T.astype(HALF)
    values[...] = jnp.zeros_like(values)

    pl.semaphore_wait(barrier, n_row + n_col - 2)

    def tile_copy(kind, sweep, d):
        return pltpu.make_async_remote_copy(
            src_ref=packed.at[kind, sweep, d],
            dst_ref=ghosts.at[kind, sweep, OPPOSITE[d]],
            send_sem=pack_send.at[kind, sweep, d],
            recv_sem=pack_recv.at[kind, sweep, OPPOSITE[d]],
            device_id=neighbours[d],
            device_id_type=MESH,
        )

    def send_tiles(kind, sweep, value):
        packed[kind, sweep] = value.astype(HALF).reshape(tiles, tile, width)
        for d in range(tiles):
            tile_copy(kind, sweep, d).start()

    def take_tiles(kind, sweep):
        for d in range(tiles):
            tile_copy(kind, sweep, d).wait_recv()
        return ghosts[kind, sweep].reshape(rim, width)

    def block_copy(sweep, step):
        return pltpu.make_async_remote_copy(
            src_ref=gather_src.at[sweep],
            dst_ref=gathered.at[sweep, col],
            send_sem=gather_send.at[sweep, step],
            recv_sem=gather_recv.at[sweep, step],
            device_id=at_col(step),
            device_id_type=MESH,
        )

    def part_copy(sweep, step):
        return pltpu.make_async_remote_copy(
            src_ref=part_src.at[sweep, lax.rem(row + step, n_row)],
            dst_ref=parts.at[sweep, row],
            send_sem=part_send.at[sweep, step],
            recv_sem=part_recv.at[sweep, step],
            device_id=at_row(step),
            device_id_type=MESH,
        )

    def every(count, act):
        def body(i, carry):
            act(i + 1)
            return carry

        lax.fori_loop(0, count - 1, body, 0)

    def sweep_once(sweep, carry):
        @pl.when(sweep == 0)
        def _():
            loads[0].wait()
            held[...] = target[...].astype(HALF)

        @pl.when(sweep > 0)
        def _():
            @pl.when(sweep == 1)
            def _():
                loads[3].wait()

            held[...] = values[...].astype(HALF)
            send_tiles(0, sweep, dot(pick[...], held[...]))
            total[...] = dot(operator[:, :own], held[...])
            margin = take_tiles(0, sweep)
            send_tiles(1, sweep, total[own:, :] + dot(operator[own:, own:], margin))
            total[:own, :] += dot(operator[:own, own:], margin)
            image = total[:own, :] + dot(spread[...], take_tiles(1, sweep))
            held[...] = (target[...] - image).astype(HALF)

        send_tiles(2, sweep, dot(pick[...], held[...]))

        @pl.when(sweep == 0)
        def _():
            loads[1].wait()
            loads[2].wait()

        total[...] = dot(inverse[:, :own], held[...])
        coarse_own = dot(basis_turned[:, :own], held[...])
        margin = take_tiles(2, sweep)
        restricted = (coarse_own + dot(basis_turned[:, own:], margin)).astype(HALF)
        gather_src[sweep] = restricted
        gathered[sweep, col] = restricted
        every(n_col, lambda step: block_copy(sweep, step).start())
        total[...] += dot(inverse[:, own:], margin)
        every(n_col, lambda step: block_copy(sweep, step).wait_recv())
        part = dot(coarse[...], gathered[sweep].reshape(n_col * level, width)).astype(HALF)
        part_src[sweep] = part.reshape(n_row, level, width)
        parts[sweep, row] = part_src[sweep, row]
        every(n_row, lambda step: part_copy(sweep, step).start())
        every(n_row, lambda step: part_copy(sweep, step).wait_recv())
        solved = jnp.sum(parts[sweep].astype(F32), axis=0).astype(HALF)
        send_tiles(3, sweep, total[own:, :] + dot(basis_ref[own:, :], solved))
        total[:own, :] += dot(basis_ref[:own, :], solved)
        values[...] += DAMPING * (total[:own, :] + dot(spread[...], take_tiles(3, sweep)))
        return carry

    lax.fori_loop(0, ITERS, sweep_once, 0)
    out_ref[...] = values[...]

    def settle(sweep, carry):
        @pl.when(sweep > 0)
        def _():
            for d in range(tiles):
                tile_copy(0, sweep, d).wait_send()
                tile_copy(1, sweep, d).wait_send()

        for d in range(tiles):
            tile_copy(2, sweep, d).wait_send()
            tile_copy(3, sweep, d).wait_send()
        every(n_col, lambda step: block_copy(sweep, step).wait_send())
        every(n_row, lambda step: part_copy(sweep, step).wait_send())
        return carry

    lax.fori_loop(0, ITERS, settle, 0)


def solution(mesh):
    n_row, n_col = mesh.shape["row"], mesh.shape["col"]

    def per_device(
        right_side, local_operator, local_inverse, coarse_basis, coarse_inverse, send_rows, send_count
    ):
        target = right_side[0, 0]
        own, width = target.shape
        basis = coarse_basis[0, 0]
        local, level = basis.shape
        rows_list = send_rows[0, 0]
        tiles, tile = rows_list.shape
        rim = tiles * tile
        turn = coarse_inverse.shape[2]
        coarse = coarse_inverse.reshape(-1, turn)
        vmem = pl.BlockSpec(memory_space=pltpu.VMEM)
        anywhere = pl.BlockSpec(memory_space=pl.ANY)
        out = pl.pallas_call(
            functools.partial(kernel, n_row, n_col),
            out_shape=jax.ShapeDtypeStruct((own, width), F32),
            in_specs=[
                anywhere, anywhere, anywhere, vmem, anywhere, vmem,
                pl.BlockSpec(memory_space=pltpu.SMEM),
            ],
            out_specs=vmem,
            scratch_shapes=[
                pltpu.VMEM((local, local), HALF),
                pltpu.VMEM((local, local), HALF),
                pltpu.VMEM(coarse.shape, HALF),
                pltpu.VMEM((own, width), F32),
                pltpu.VMEM((level, local), HALF),
                pltpu.VMEM((rim, own), HALF),
                pltpu.VMEM((own, rim), HALF),
                pltpu.VMEM((local, width), F32),
                pltpu.VMEM((own, width), F32),
                pltpu.VMEM((own, width), HALF),
                pltpu.VMEM((4, ITERS, tiles, tile, width), HALF),
                pltpu.VMEM((4, ITERS, tiles, tile, width), HALF),
                pltpu.VMEM((ITERS, level, width), HALF),
                pltpu.VMEM((ITERS, n_col, level, width), HALF),
                pltpu.VMEM((ITERS, n_row, level, width), HALF),
                pltpu.VMEM((ITERS, n_row, level, width), HALF),
                pltpu.SemaphoreType.DMA((4,)),
                pltpu.SemaphoreType.DMA((4, ITERS, tiles)),
                pltpu.SemaphoreType.DMA((4, ITERS, tiles)),
                pltpu.SemaphoreType.DMA((ITERS, n_col)),
                pltpu.SemaphoreType.DMA((ITERS, n_col)),
                pltpu.SemaphoreType.DMA((ITERS, n_row)),
                pltpu.SemaphoreType.DMA((ITERS, n_row)),
            ],
            compiler_params=pltpu.CompilerParams(
                collective_id=0, has_side_effects=True, vmem_limit_bytes=60 * 1024 * 1024
            ),
        )(
            target,
            local_operator[0, 0],
            local_inverse[0, 0],
            basis,
            coarse,
            rows_list,
            send_count[0],
        )
        return out[None, None]

    return jax.shard_map(
        per_device,
        mesh=mesh,
        in_specs=(
            P("row", "col", None, None),
            P("row", "col", None, None),
            P("row", "col", None, None),
            P("row", "col", None, None),
            P(None, "col", "row"),
            P("row", "col", None, None),
            P("row", "col", None),
        ),
        out_specs=P("row", "col", None, None),
        check_vma=False,
    )
```

time: 584 us -> 132 us (0.23); the launches traced: 578 us -> 131 us
  waiting for transfers between devices: 295 us -> 0 us
  Pallas kernels: 0 us -> 127 us
  starting transfers between devices: 117 us -> 0 us
  blocking collectives: 57.1 us -> 0 us
  other arithmetic: 36 us -> 0 us
  matrix products: 27.8 us -> 0 us
  local copies, waits for them, and re-layouts: 30.1 us -> 4.08 us
  between operations: 14.1 us -> 0.01 us
    unnamed x6 -> x0, waiting for transfers between devices: 264 us -> none
    pallas_call x0 -> x1, Pallas kernels: none -> 127 us  [per_device(): pl.pallas_call(functools.partial(kernel, n_row, n_col), out_shape=jax.Sha...]
    ppermute x40 -> x0, starting transfers between devices: 117 us -> none  [passed_along(): return lax.ppermute(shard, axis, pairs)]
    all_gather x3 -> x0, blocking collectives: 57.1 us -> none  [per_device(): block_rows = lax.all_gather(restricted, 'col', axis=0, tiled=True)]
    ppermute x40 -> x0, waiting for transfers between devices: 31 us -> none  [passed_along(): return lax.ppermute(shard, axis, pairs)]
    dot_general x14 -> x0, matrix products: 27.8 us -> none  [the longest x3 13.8 us: per_device(): jnp.dot(inverse, residual_local, preferred_element_type=jnp.float32)]
    scatter-add x5 -> x0, other arithmetic: 21.8 us -> none  [owner_sum(): summed = jnp.zeros((own_rows, columns), jnp.float32).at[flat_rows].add(we...]
    slice x15 -> x0, local copies, waits for them, and re-layouts: 13.1 us -> none  [the longest x10 12.9 us: owner_sum(): return local_terms[:own_rows] + summed]
  transfers between devices with their start and end apart: 43 -> 0, of which waited for: 13 -> 0; matrix products, arithmetic and copies ran while one was open for 5% -> 0% of each run, Pallas kernels for 0% -> 0%
where the time goes in v1:
time: 132 us; the launch traced here: 131 us
  Pallas kernels  127 us (96%)
  local copies, waits for them, and re-layouts  4.08 us (3%)
    pallas_call x1, Pallas kernels, per_device(): pl.pallas_call(functools.partial(kernel, n_row, n_col), out_shape=jax.Sha...  127 us
    unnamed x2, local copies, waits for them, and re-layouts  4.08 us

profile of v1, /device:TPU:1, one launch (start us, length us, event | category | flops | bytes accessed | tf_op | source)
XLA Modules:
  0.0 131.5 jit_solution(15359588907506591690)
XLA Ops:
  0.0 1.8 %copy.8 = bf16[1,1,1536,32]{3,2,1,0:T(8,128)(2,1)} copy(bf16[1,1,1536,32]{2,3,1,0:T(8,128)(2,1)} %param.10) | data formatting | bytes 196608 | tf_op args[3]
  1.8 127.4 %shard_map.73 = f32[1024,256]{1,0:T(8,128)} custom-call(f32[1024,256]{1,0:T(8,128)} %bitcast.12, bf16[1536,1536]{1,0:T(8,128)(2,1)} %bitcast.8, bf16[1536,1536]{1,0:T(8,128)(2,1)} %bitcast.9, bf16[1536,32]{1,0:T(8,128)(2,1)} %bitcast.11, bf16[512,512]{1,0:T(8,128)(2,1)} %bitcast.13, s32[4,128]{1,0:T(4,128)} %bitcast.14, s32[1,4]{1,0:T(1,128)} %bitcast.15), custom_call_target="tpu_custom_call" | custom-call | tf_op jit(solution)/shard_map/pallas_call | solution.py:222
  129.2 2.3 %copy.10 = f32[1,1,1024,256]{3,2,1,0:T(8,128)} copy(f32[1,1,1024,256]{3,2,1,0:T(8,128)} %bitcast.10) | data formatting | bytes 2097152

commit v2 on v1

v2 whole, which is shorter than its diff:
```python
import functools

import jax
import jax.numpy as jnp
from jax import lax
from jax.experimental import pallas as pl
from jax.experimental.pallas import tpu as pltpu
from jax.sharding import PartitionSpec as P

ITERS = 3
DAMPING = 0.5
MESH = pl.DeviceIdType.MESH
OPPOSITE = (1, 0, 3, 2)
F32 = jnp.float32
HALF = jnp.bfloat16
STENCIL = (
    (0, 0), (-1, 0), (1, 0), (0, -1), (0, 1),
    (-2, 0), (2, 0), (-1, -1), (-1, 1), (1, -1), (1, 1), (0, -2), (0, 2),
)
NEAR = 5
OUTER_FIRST = tuple(range(NEAR, len(STENCIL))) + tuple(range(1, NEAR))


def stencil_index(down, right):
    return STENCIL.index((down, right))


def mirrored(k):
    return stencil_index(-STENCIL[k][0], -STENCIL[k][1])


def dot(left, right):
    return jnp.dot(left, right, preferred_element_type=F32)


def dot_turned(left, right):
    return lax.dot_general(left, right, (((1,), (1,)), ((), ())), preferred_element_type=F32)


def ring_steps(n_row, n_col):
    fast = 4
    half = n_col // 2
    rows = [(a, b) for a in range(n_row // fast) for b in range(fast)][1:]

    def row_hops(o):
        return 2 * min(o[0], n_row // fast - o[0]) + min(o[1], fast - o[1])

    cols = [(a, b, c) for a in range(2) for b in range(half // 2) for c in range(2)][1:]

    def col_hops(o):
        return o[0] + min(o[1], half // 2 - o[1])

    return sorted(rows, key=row_hops, reverse=True), sorted(cols, key=col_hops, reverse=True)


def kernel(
    n_row, n_col,
    target_hbm, operator_hbm, inverse_hbm, basis_ref, coarse_hbm, rows_ref, counts_ref,
    out_ref,
    operator, inverse, coarse, target, pick, spread, total, image, image_half, values, held, first,
    packed, ghosts, gather_src, gathered, part_src, parts, sums_src, sums, levels,
    basis_src, basis_tiles, wide_src, wide_tiles, assembled, psi, near_image, far_image,
    load_sem, pack_send, pack_recv, gather_send, gather_recv, part_send, part_recv,
    sums_send, sums_recv, level_send, level_recv, setup_send, setup_recv,
):
    own, width = target.shape
    tiles, tile = rows_ref.shape
    rim = tiles * tile
    level = basis_ref.shape[0]
    near = NEAR * level
    row = lax.axis_index("row")
    col = lax.axis_index("col")
    row_steps, col_steps = ring_steps(n_row, n_col)

    def at(down, right):
        return (
            lax.rem(row + (down + n_row), n_row) if down else row,
            lax.rem(col + (right + n_col), n_col) if right else col,
        )

    def row_peer(step):
        a, b = step
        return lax.rem(lax.div(row, 4) + a, n_row // 4) * 4 + lax.rem(lax.rem(row, 4) + b, 4)

    def col_peer(step):
        a, b, c = step
        quarter = n_col // 4
        return (
            lax.rem(lax.div(col, n_col // 2) + a, 2) * (n_col // 2)
            + lax.rem(lax.rem(lax.div(col, 2), quarter) + b, quarter) * 2
            + lax.rem(lax.rem(col, 2) + c, 2)
        )

    neighbours = [at(*STENCIL[1 + d]) for d in range(tiles)]

    loads = [
        pltpu.make_async_copy(source, place, load_sem.at[i])
        for i, (source, place) in enumerate(
            (
                (target_hbm, target),
                (inverse_hbm, inverse),
                (coarse_hbm, coarse),
                (operator_hbm, operator),
            )
        )
    ]
    for load in loads:
        load.start()

    barrier = pltpu.get_barrier_semaphore()
    greeted = 0
    for step in row_steps:
        pl.semaphore_signal(barrier, inc=1, device_id=(row_peer(step), col), device_id_type=MESH)
        greeted += 1
    for step in col_steps:
        pl.semaphore_signal(barrier, inc=1, device_id=(row, col_peer(step)), device_id_type=MESH)
        greeted += 1
    for down, right in STENCIL:
        if down and right:
            pl.semaphore_signal(barrier, inc=1, device_id=at(down, right), device_id_type=MESH)
            greeted += 1

    def tile_copy(kind, sweep, d):
        return pltpu.make_async_remote_copy(
            src_ref=packed.at[kind, sweep, d],
            dst_ref=ghosts.at[kind, sweep, OPPOSITE[d]],
            send_sem=pack_send.at[kind, sweep, d],
            recv_sem=pack_recv.at[kind, sweep, OPPOSITE[d]],
            device_id=neighbours[d],
            device_id_type=MESH,
        )

    def store_tiles(kind, sweep, value):
        packed[kind, sweep] = value.astype(HALF).reshape(tiles, tile, width)

    def start_tiles(kind, sweep):
        for d in range(tiles):
            tile_copy(kind, sweep, d).start()

    def send_tiles(kind, sweep, value):
        store_tiles(kind, sweep, value)
        start_tiles(kind, sweep)

    def take_tiles(kind, sweep):
        for d in range(tiles):
            tile_copy(kind, sweep, d).wait_recv()
        return ghosts[kind, sweep].reshape(rim, width)

    def setup_copy(stage, source, place, d):
        return pltpu.make_async_remote_copy(
            src_ref=source.at[d],
            dst_ref=place.at[OPPOSITE[d]],
            send_sem=setup_send.at[stage, d],
            recv_sem=setup_recv.at[stage, OPPOSITE[d]],
            device_id=neighbours[d],
            device_id_type=MESH,
        )

    def basis_copy(d):
        return setup_copy(0, basis_src, basis_tiles, d)

    def wide_copy(d):
        return setup_copy(1, wide_src, wide_tiles, d)

    def block_copy(sweep, i):
        return pltpu.make_async_remote_copy(
            src_ref=gather_src.at[sweep],
            dst_ref=gathered.at[sweep, col],
            send_sem=gather_send.at[sweep, i],
            recv_sem=gather_recv.at[sweep, i],
            device_id=(row, col_peer(col_steps[i])),
            device_id_type=MESH,
        )

    def part_copy(sweep, i):
        peer = row_peer(row_steps[i])
        return pltpu.make_async_remote_copy(
            src_ref=part_src.at[sweep, peer],
            dst_ref=parts.at[sweep, row],
            send_sem=part_send.at[sweep, i],
            recv_sem=part_recv.at[sweep, i],
            device_id=(peer, col),
            device_id_type=MESH,
        )

    def sum_copy(sweep, k):
        return pltpu.make_async_remote_copy(
            src_ref=sums_src.at[sweep, k],
            dst_ref=sums.at[sweep, mirrored(k)],
            send_sem=sums_send.at[sweep, k],
            recv_sem=sums_recv.at[sweep, mirrored(k)],
            device_id=at(*STENCIL[k]),
            device_id_type=MESH,
        )

    def level_copy(sweep, k):
        return pltpu.make_async_remote_copy(
            src_ref=levels.at[sweep, 0],
            dst_ref=levels.at[sweep, mirrored(k)],
            send_sem=level_send.at[sweep, k],
            recv_sem=level_recv.at[sweep, mirrored(k)],
            device_id=at(*STENCIL[k]),
            device_id_type=MESH,
        )

    def send_restricted(sweep, value):
        restricted = value.astype(HALF)
        gather_src[sweep] = restricted
        gathered[sweep, col] = restricted
        for i in range(n_col - 1):
            block_copy(sweep, i).start()

    def solve_part(sweep):
        for i in range(n_col - 1):
            block_copy(sweep, i).wait_recv()
        part = dot(coarse[...], gathered[sweep].reshape(n_col * level, width)).astype(HALF)
        part_src[sweep] = part.reshape(n_row, level, width)
        for i in range(n_row - 1):
            part_copy(sweep, i).start()
        parts[sweep, row] = part_src[sweep, row]

    def solve_rest(sweep, far):
        for i in range(n_row - 1):
            part_copy(sweep, i).wait_recv()
        levels[sweep, 0] = jnp.sum(parts[sweep].astype(F32), axis=0).astype(HALF)

        def outer():
            for k in range(NEAR, len(STENCIL)):
                level_copy(sweep, k).start()

        if far is True:
            outer()
        else:
            pl.when(far)(outer)
        for k in range(1, NEAR):
            level_copy(sweep, k).start()

    place = lax.broadcasted_iota(jnp.int32, (1, tile), 1)
    square = lax.broadcasted_iota(jnp.int32, (tile, tile), 0) == lax.broadcasted_iota(
        jnp.int32, (tile, tile), 1
    )
    lists = [
        jnp.where(place < counts_ref[0, d], rows_ref[d : d + 1, :], -1).astype(F32)
        for d in range(tiles)
    ]
    along = lax.broadcasted_iota(jnp.int32, (tile, own), 1).astype(F32)
    for d in range(tiles):
        upright = jnp.sum(
            jnp.where(square, jnp.broadcast_to(lists[d], (tile, tile)), 0.0), axis=1, keepdims=True
        )
        pick[d * tile : (d + 1) * tile, :] = jnp.where(along == upright, 1.0, 0.0).astype(HALF)
        basis_src[d] = basis_ref[:, own + d * tile : own + (d + 1) * tile]
    loads[0].wait()
    held[...] = target[...].astype(HALF)
    store_tiles(2, 0, dot(pick[...], held[...]))

    pl.semaphore_wait(barrier, greeted)

    start_tiles(2, 0)
    for d in range(tiles):
        basis_copy(d).start()
    down = lax.broadcasted_iota(jnp.int32, (own, tile), 0).astype(F32)
    for d in range(tiles):
        spread[:, d * tile : (d + 1) * tile] = jnp.where(down == lists[d], 1.0, 0.0).astype(HALF)
    assembled[...] = jnp.zeros_like(assembled)
    coarse_own = dot(basis_ref[:, :own], held[...])
    loads[1].wait()
    total[...] = dot(inverse[:, :own], held[...])
    margin = take_tiles(2, 0)
    first[...] = coarse_own + dot(basis_ref[:, own:], margin)
    send_restricted(0, first[...])
    total[...] += dot(inverse[:, own:], margin)
    send_tiles(3, 0, total[own:, :])

    assembled[:level, :own] = basis_ref[:, :own]
    for d in range(tiles):
        basis_copy(d).wait_recv()
    for d in range(tiles):
        assembled[(1 + d) * level : (2 + d) * level, :own] = dot(
            basis_tiles[d], pick[d * tile : (d + 1) * tile, :]
        ).astype(HALF)
    wide = dot(assembled[:near, :own], spread[...]).astype(HALF)
    for d in range(tiles):
        wide_src[d] = wide[:, d * tile : (d + 1) * tile]
    for d in range(tiles):
        wide_copy(d).start()

    loads[2].wait()
    solve_part(0)
    values[...] = DAMPING * (total[:own, :] + dot(spread[...], take_tiles(3, 0)))
    held[...] = values[...].astype(HALF)
    send_tiles(0, 0, dot(pick[...], held[...]))
    loads[3].wait()
    image[...] = dot(operator[:, :own], held[...])
    psi[...] = assembled[:near, :own].astype(F32).T.astype(HALF)
    for d in range(tiles):
        wide_copy(d).wait_recv()
    for d in range(tiles):
        for e in range(NEAR):
            k = stencil_index(
                STENCIL[1 + d][0] + STENCIL[e][0], STENCIL[1 + d][1] + STENCIL[e][1]
            )
            assembled[k * level : (k + 1) * level, own + d * tile : own + (d + 1) * tile] = (
                wide_tiles[d, e * level : (e + 1) * level, :]
            )
    near_image[...] = dot_turned(operator[...], assembled[:near, :]).astype(HALF)
    far_image[...] = dot_turned(operator[:, own:], assembled[near:, own:]).astype(HALF)
    image[...] += dot(operator[:, own:], take_tiles(0, 0))
    solve_rest(0, True)

    def take_near(sweep):
        for k in range(1, NEAR):
            level_copy(sweep, k).wait_recv()
        return levels[sweep, :NEAR].reshape(near, width)

    def sweep_once(sweep, carry):
        before = sweep - 1
        goes_on = sweep < ITERS - 1
        for k in range(NEAR, len(STENCIL)):
            level_copy(before, k).wait_recv()
        around = take_near(before)
        beyond = levels[before, NEAR:].reshape(-1, width)
        image[...] += DAMPING * (dot(near_image[...], around) + dot(far_image[...], beyond))
        image_half[...] = image[...].astype(HALF)
        near_sums = dot(assembled[:near, :], image_half[...])
        far_sums = dot(assembled[near:, own:], image_half[own:, :])
        sums_src[sweep, :NEAR] = near_sums.astype(HALF).reshape(NEAR, level, width)
        sums_src[sweep, NEAR:] = far_sums.astype(HALF).reshape(-1, level, width)
        for k in OUTER_FIRST:
            sum_copy(sweep, k).start()
        packed[1, sweep] = image_half[own:, :].reshape(tiles, tile, width)
        start_tiles(1, sweep)
        values[...] += DAMPING * dot(psi[...], around)

        for k in range(1, len(STENCIL)):
            sum_copy(sweep, k).wait_recv()
        sums[sweep, 0] = sums_src[sweep, 0]
        send_restricted(sweep, first[...] - jnp.sum(sums[sweep].astype(F32), axis=0))
        returned = take_tiles(1, sweep)
        held[...] = (target[...] - image[:own, :] - dot(spread[...], returned)).astype(HALF)
        send_tiles(2, sweep, dot(pick[...], held[...]))
        total[...] = dot(inverse[:, :own], held[...])
        solve_part(sweep)
        total[...] += dot(inverse[:, own:], take_tiles(2, sweep))
        send_tiles(3, sweep, total[own:, :])
        values[...] += DAMPING * (total[:own, :] + dot(spread[...], take_tiles(3, sweep)))

        @pl.when(goes_on)
        def _():
            held[...] = values[...].astype(HALF)
            send_tiles(0, sweep, dot(pick[...], held[...]))

        solve_rest(sweep, goes_on)

        @pl.when(goes_on)
        def _():
            image[...] = dot(operator[:, :own], held[...])
            image[...] += dot(operator[:, own:], take_tiles(0, sweep))

        return carry

    lax.fori_loop(1, ITERS, sweep_once, 0)
    out_ref[...] = values[...] + DAMPING * dot(psi[...], take_near(ITERS - 1))

    for d in range(tiles):
        basis_copy(d).wait_send()
        wide_copy(d).wait_send()

    def settle(sweep, carry):
        for d in range(tiles):
            tile_copy(2, sweep, d).wait_send()
            tile_copy(3, sweep, d).wait_send()
        for i in range(n_col - 1):
            block_copy(sweep, i).wait_send()
        for i in range(n_row - 1):
            part_copy(sweep, i).wait_send()
        for k in range(1, NEAR):
            level_copy(sweep, k).wait_send()

        @pl.when(sweep > 0)
        def _():
            for d in range(tiles):
                tile_copy(1, sweep, d).wait_send()
            for k in range(1, len(STENCIL)):
                sum_copy(sweep, k).wait_send()

        @pl.when(sweep < ITERS - 1)
        def _():
            for d in range(tiles):
                tile_copy(0, sweep, d).wait_send()
            for k in range(NEAR, len(STENCIL)):
                level_copy(sweep, k).wait_send()

        return carry

    lax.fori_loop(0, ITERS, settle, 0)


def solution(mesh):
    n_row, n_col = mesh.shape["row"], mesh.shape["col"]

    def per_device(
        right_side, local_operator, local_inverse, coarse_basis, coarse_inverse, send_rows, send_count
    ):
        target = right_side[0, 0]
        own, width = target.shape
        basis = coarse_basis[0, 0].T
        level, local = basis.shape
        rows_list = send_rows[0, 0]
        tiles, tile = rows_list.shape
        rim = tiles * tile
        coarse = coarse_inverse.reshape(-1, coarse_inverse.shape[2])
        points = len(STENCIL)
        near, far = NEAR * level, (points - NEAR) * level
        vmem = pl.BlockSpec(memory_space=pltpu.VMEM)
        anywhere = pl.BlockSpec(memory_space=pl.ANY)
        dma = pltpu.SemaphoreType.DMA
        out = pl.pallas_call(
            functools.partial(kernel, n_row, n_col),
            out_shape=jax.ShapeDtypeStruct((own, width), F32),
            in_specs=[
                anywhere, anywhere, anywhere, vmem, anywhere, vmem,
                pl.BlockSpec(memory_space=pltpu.SMEM),
            ],
            out_specs=vmem,
            scratch_shapes=[
                pltpu.VMEM((local, local), HALF),
                pltpu.VMEM((local, local), HALF),
                pltpu.VMEM(coarse.shape, HALF),
                pltpu.VMEM((own, width), F32),
                pltpu.VMEM((rim, own), HALF),
                pltpu.VMEM((own, rim), HALF),
                pltpu.VMEM((local, width), F32),
                pltpu.VMEM((local, width), F32),
                pltpu.VMEM((local, width), HALF),
                pltpu.VMEM((own, width), F32),
                pltpu.VMEM((own, width), HALF),
                pltpu.VMEM((level, width), F32),
                pltpu.VMEM((4, ITERS, tiles, tile, width), HALF),
                pltpu.VMEM((4, ITERS, tiles, tile, width), HALF),
                pltpu.VMEM((ITERS, level, width), HALF),
                pltpu.VMEM((ITERS, n_col, level, width), HALF),
                pltpu.VMEM((ITERS, n_row, level, width), HALF),
                pltpu.VMEM((ITERS, n_row, level, width), HALF),
                pltpu.VMEM((ITERS, points, level, width), HALF),
                pltpu.VMEM((ITERS, points, level, width), HALF),
                pltpu.VMEM((ITERS, points, level, width), HALF),
                pltpu.VMEM((tiles, level, tile), HALF),
                pltpu.VMEM((tiles, level, tile), HALF),
                pltpu.VMEM((tiles, near, tile), HALF),
                pltpu.VMEM((tiles, near, tile), HALF),
                pltpu.VMEM((near + far, local), HALF),
                pltpu.VMEM((own, near), HALF),
                pltpu.VMEM((local, near), HALF),
                pltpu.VMEM((local, far), HALF),
                dma((4,)),
                dma((4, ITERS, tiles)),
                dma((4, ITERS, tiles)),
                dma((ITERS, n_col - 1)),
                dma((ITERS, n_col - 1)),
                dma((ITERS, n_row - 1)),
                dma((ITERS, n_row - 1)),
                dma((ITERS, points)),
                dma((ITERS, points)),
                dma((ITERS, points)),
                dma((ITERS, points)),
                dma((2, tiles)),
                dma((2, tiles)),
            ],
            compiler_params=pltpu.CompilerParams(
                collective_id=0, has_side_effects=True, vmem_limit_bytes=60 * 1024 * 1024
            ),
        )(
            target,
            local_operator[0, 0],
            local_inverse[0, 0],
            basis,
            coarse,
            rows_list,
            send_count[0],
        )
        return out[None, None]

    return jax.shard_map(
        per_device,
        mesh=mesh,
        in_specs=(
            P("row", "col", None, None),
            P("row", "col", None, None),
            P("row", "col", None, None),
            P("row", "col", None, None),
            P(None, "col", "row"),
            P("row", "col", None, None),
            P("row", "col", None),
        ),
        out_specs=P("row", "col", None, None),
        check_vma=False,
    )
```

time: 132 us -> 125 us (0.947)
  Pallas kernels: 127 us -> 122 us
  local copies, waits for them, and re-layouts: 4.08 us -> 2.26 us
    pallas_call x1, Pallas kernels: 127 us -> 122 us  [per_device(): pl.pallas_call(functools.partial(kernel, n_row, n_col), out_shape=jax.Sha...]
    unnamed x2 -> x1, local copies, waits for them, and re-layouts: 4.08 us -> 2.26 us
where the time goes in v2:
time: 125 us
  Pallas kernels  122 us (98%)
  local copies, waits for them, and re-layouts  2.26 us (2%)
    pallas_call x1, Pallas kernels, per_device(): pl.pallas_call(functools.partial(kernel, n_row, n_col), out_shape=jax.Sha...  122 us

profile of v2, /device:TPU:1, one launch (start us, length us, event | category | flops | bytes accessed | tf_op | source)
XLA Modules:
  0.0 124.7 jit_solution(9273429558506852106)
XLA Ops:
  0.0 122.5 %shard_map.73 = f32[1024,256]{1,0:T(8,128)} custom-call(f32[1024,256]{1,0:T(8,128)} %bitcast.13, bf16[1536,1536]{1,0:T(8,128)(2,1)} %bitcast.10, bf16[1536,1536]{1,0:T(8,128)(2,1)} %bitcast.11, bf16[32,1536]{1,0:T(8,128)(2,1)} %bitcast.15, bf16[512,512]{1,0:T(8,128)(2,1)} %bitcast.14, s32[4,128]{1,0:T(4,128)} %bitcast.16, s32[1,4]{1,0:T(1,128)} %bitcast.17), custom_call_target="tpu_custom_call" | custom-call | tf_op jit(solution)/shard_map/pallas_call | solution.py:418
  122.5 2.3 %copy.9 = f32[1,1,1024,256]{3,2,1,0:T(8,128)} copy(f32[1,1,1024,256]{3,2,1,0:T(8,128)} %bitcast.12) | data formatting | bytes 2097152

commit v3 on v2

--- a/solution.py
+++ b/solution.py
@@ -56,11 +56,12 @@
 def kernel(
     n_row, n_col,
     target_hbm, operator_hbm, inverse_hbm, basis_ref, coarse_hbm, rows_ref, counts_ref,
-    out_ref,
-    operator, inverse, coarse, target, pick, spread, total, image, image_half, values, held, first,
+    values_out, psi_out, around_ref,
+    operator, inverse, coarse, target, pick, spread, cross, ahead, total, image, values, held, first,
     packed, ghosts, gather_src, gathered, part_src, parts, sums_src, sums, levels,
     basis_src, basis_tiles, wide_src, wide_tiles, assembled, psi, near_image, far_image,
-    load_sem, pack_send, pack_recv, gather_send, gather_recv, part_send, part_recv,
+    ghost_sums, near_sums, far_sums, own_sums,
+    load_sem, store_sem, pack_send, pack_recv, gather_send, gather_recv, part_send, part_recv,
     sums_send, sums_recv, level_send, level_recv, setup_send, setup_recv,
 ):
     own, width = target.shape
@@ -235,6 +236,15 @@
         for k in range(1, NEAR):
             level_copy(sweep, k).start()
 
+    def sums_of_own():
+        own_sums[:near, :] = dot(assembled[:near, :], image[...].astype(HALF))
+        own_sums[near:, :] = dot(assembled[near:, own:], image[own:, :].astype(HALF))
+
+    def pick_ahead(value):
+        coarser = value.astype(HALF)
+        finer = (value - coarser.astype(F32)).astype(HALF)
+        ahead[...] = dot(pick[...], coarser) + dot(pick[...], finer)
+
     place = lax.broadcasted_iota(jnp.int32, (1, tile), 1)
     square = lax.broadcasted_iota(jnp.int32, (tile, tile), 0) == lax.broadcasted_iota(
         jnp.int32, (tile, tile), 1
@@ -262,6 +272,7 @@
     down = lax.broadcasted_iota(jnp.int32, (own, tile), 0).astype(F32)
     for d in range(tiles):
         spread[:, d * tile : (d + 1) * tile] = jnp.where(down == lists[d], 1.0, 0.0).astype(HALF)
+    cross[...] = dot(pick[...], spread[...]).astype(HALF)
     assembled[...] = jnp.zeros_like(assembled)
     coarse_own = dot(basis_ref[:, :own], held[...])
     loads[1].wait()
@@ -269,8 +280,8 @@
     margin = take_tiles(2, 0)
     first[...] = coarse_own + dot(basis_ref[:, own:], margin)
     send_restricted(0, first[...])
-    total[...] += dot(inverse[:, own:], margin)
-    send_tiles(3, 0, total[own:, :])
+    send_tiles(3, 0, total[own:, :] + dot(inverse[own:, own:], margin))
+    total[:own, :] += dot(inverse[:own, own:], margin)
 
     assembled[:level, :own] = basis_ref[:, :own]
     for d in range(tiles):
@@ -287,12 +298,17 @@
 
     loads[2].wait()
     solve_part(0)
-    values[...] = DAMPING * (total[:own, :] + dot(spread[...], take_tiles(3, 0)))
+    values[...] = DAMPING * total[:own, :]
+    pick_ahead(values[...])
+    returned = take_tiles(3, 0)
+    send_tiles(0, 0, ahead[...] + DAMPING * dot(cross[...], returned))
+    values[...] += DAMPING * dot(spread[...], returned)
     held[...] = values[...].astype(HALF)
-    send_tiles(0, 0, dot(pick[...], held[...]))
     loads[3].wait()
     image[...] = dot(operator[:, :own], held[...])
     psi[...] = assembled[:near, :own].astype(F32).T.astype(HALF)
+    psi_store = pltpu.make_async_copy(psi, psi_out, store_sem.at[0])
+    psi_store.start()
     for d in range(tiles):
         wide_copy(d).wait_recv()
     for d in range(tiles):
@@ -305,8 +321,17 @@
             )
     near_image[...] = dot_turned(operator[...], assembled[:near, :]).astype(HALF)
     far_image[...] = dot_turned(operator[:, own:], assembled[near:, own:]).astype(HALF)
-    image[...] += dot(operator[:, own:], take_tiles(0, 0))
     solve_rest(0, True)
+    ghost_sums[:near, :] = dot(assembled[:near, :], operator[:, own:]).astype(HALF)
+    ghost_sums[near:, :] = dot(assembled[near:, own:], operator[own:, own:]).astype(HALF)
+    near_sums[:near, :] = dot(assembled[:near, :], near_image[...]).astype(HALF)
+    near_sums[near:, :] = dot(assembled[near:, own:], near_image[own:, :]).astype(HALF)
+    far_sums[:near, :] = dot(assembled[:near, :], far_image[...]).astype(HALF)
+    far_sums[near:, :] = dot(assembled[near:, own:], far_image[own:, :]).astype(HALF)
+    sums_of_own()
+
+    def values_store():
+        return pltpu.make_async_copy(values, values_out, store_sem.at[1])
 
     def take_near(sweep):
         for k in range(1, NEAR):
@@ -316,20 +341,28 @@
     def sweep_once(sweep, carry):
         before = sweep - 1
         goes_on = sweep < ITERS - 1
+        margin = take_tiles(0, before)
+        image[own:, :] += dot(operator[own:, own:], margin)
+        own_sums[...] += dot(ghost_sums[...], margin)
         for k in range(NEAR, len(STENCIL)):
             level_copy(before, k).wait_recv()
         around = take_near(before)
         beyond = levels[before, NEAR:].reshape(-1, width)
-        image[...] += DAMPING * (dot(near_image[...], around) + dot(far_image[...], beyond))
-        image_half[...] = image[...].astype(HALF)
-        near_sums = dot(assembled[:near, :], image_half[...])
-        far_sums = dot(assembled[near:, own:], image_half[own:, :])
-        sums_src[sweep, :NEAR] = near_sums.astype(HALF).reshape(NEAR, level, width)
-        sums_src[sweep, NEAR:] = far_sums.astype(HALF).reshape(-1, level, width)
+        owed = own_sums[...] + DAMPING * (dot(near_sums[...], around) + dot(far_sums[...], beyond))
+        sums_src[sweep] = owed.astype(HALF).reshape(len(STENCIL), level, width)
         for k in OUTER_FIRST:
             sum_copy(sweep, k).start()
-        packed[1, sweep] = image_half[own:, :].reshape(tiles, tile, width)
-        start_tiles(1, sweep)
+        send_tiles(
+            1,
+            sweep,
+            image[own:, :]
+            + DAMPING * (dot(near_image[own:, :], around) + dot(far_image[own:, :], beyond)),
+        )
+        image[:own, :] += dot(operator[:own, own:], margin) + DAMPING * (
+            dot(near_image[:own, :], around) + dot(far_image[:own, :], beyond)
+        )
+        total[:own, :] = target[...] - image[:own, :]
+        pick_ahead(total[:own, :])
         values[...] += DAMPING * dot(psi[...], around)
 
         for k in range(1, len(STENCIL)):
@@ -337,30 +370,43 @@
         sums[sweep, 0] = sums_src[sweep, 0]
         send_restricted(sweep, first[...] - jnp.sum(sums[sweep].astype(F32), axis=0))
         returned = take_tiles(1, sweep)
-        held[...] = (target[...] - image[:own, :] - dot(spread[...], returned)).astype(HALF)
-        send_tiles(2, sweep, dot(pick[...], held[...]))
+        send_tiles(2, sweep, ahead[...] - dot(cross[...], returned))
+        held[...] = (total[:own, :] - dot(spread[...], returned)).astype(HALF)
         total[...] = dot(inverse[:, :own], held[...])
         solve_part(sweep)
-        total[...] += dot(inverse[:, own:], take_tiles(2, sweep))
-        send_tiles(3, sweep, total[own:, :])
-        values[...] += DAMPING * (total[:own, :] + dot(spread[...], take_tiles(3, sweep)))
+        arrived = take_tiles(2, sweep)
+        send_tiles(3, sweep, total[own:, :] + dot(inverse[own:, own:], arrived))
+        values[...] += DAMPING * (total[:own, :] + dot(inverse[:own, own:], arrived))
 
         @pl.when(goes_on)
         def _():
-            held[...] = values[...].astype(HALF)
-            send_tiles(0, sweep, dot(pick[...], held[...]))
+            pick_ahead(values[...])
 
         solve_rest(sweep, goes_on)
+
+        returned = take_tiles(3, sweep)
 
         @pl.when(goes_on)
         def _():
-            image[...] = dot(operator[:, :own], held[...])
-            image[...] += dot(operator[:, own:], take_tiles(0, sweep))
+            send_tiles(0, sweep, ahead[...] + DAMPING * dot(cross[...], returned))
+
+        values[...] += DAMPING * dot(spread[...], returned)
+
+        @pl.when(sweep == ITERS - 1)
+        def _():
+            values_store().start()
+
+        @pl.when(goes_on)
+        def _():
+            image[...] = dot(operator[:, :own], values[...].astype(HALF))
+            sums_of_own()
 
         return carry
 
     lax.fori_loop(1, ITERS, sweep_once, 0)
-    out_ref[...] = values[...] + DAMPING * dot(psi[...], take_near(ITERS - 1))
+    around_ref[...] = take_near(ITERS - 1)
+    psi_store.wait()
+    values_store().wait()
 
     for d in range(tiles):
         basis_copy(d).wait_send()
@@ -415,14 +461,18 @@
         vmem = pl.BlockSpec(memory_space=pltpu.VMEM)
         anywhere = pl.BlockSpec(memory_space=pl.ANY)
         dma = pltpu.SemaphoreType.DMA
-        out = pl.pallas_call(
+        values, psi, around = pl.pallas_call(
             functools.partial(kernel, n_row, n_col),
-            out_shape=jax.ShapeDtypeStruct((own, width), F32),
+            out_shape=(
+                jax.ShapeDtypeStruct((own, width), F32),
+                jax.ShapeDtypeStruct((own, near), HALF),
+                jax.ShapeDtypeStruct((near, width), HALF),
+            ),
             in_specs=[
                 anywhere, anywhere, anywhere, vmem, anywhere, vmem,
                 pl.BlockSpec(memory_space=pltpu.SMEM),
             ],
-            out_specs=vmem,
+            out_specs=(anywhere, anywhere, vmem),
             scratch_shapes=[
                 pltpu.VMEM((local, local), HALF),
                 pltpu.VMEM((local, local), HALF),
@@ -430,9 +480,10 @@
                 pltpu.VMEM((own, width), F32),
                 pltpu.VMEM((rim, own), HALF),
                 pltpu.VMEM((own, rim), HALF),
+                pltpu.VMEM((rim, rim), HALF),
+                pltpu.VMEM((rim, width), F32),
                 pltpu.VMEM((local, width), F32),
                 pltpu.VMEM((local, width), F32),
-                pltpu.VMEM((local, width), HALF),
                 pltpu.VMEM((own, width), F32),
                 pltpu.VMEM((own, width), HALF),
                 pltpu.VMEM((level, width), F32),
@@ -453,7 +504,12 @@
                 pltpu.VMEM((own, near), HALF),
                 pltpu.VMEM((local, near), HALF),
                 pltpu.VMEM((local, far), HALF),
+                pltpu.VMEM((near + far, rim), HALF),
+                pltpu.VMEM((near + far, near), HALF),
+                pltpu.VMEM((near + far, far), HALF),
+                pltpu.VMEM((near + far, width), F32),
                 dma((4,)),
+                dma((2,)),
                 dma((4, ITERS, tiles)),
                 dma((4, ITERS, tiles)),
                 dma((ITERS, n_col - 1)),
@@ -479,7 +535,7 @@
             rows_list,
             send_count[0],
         )
-        return out[None, None]
+        return (values + DAMPING * dot(psi, around))[None, None]
 
     return jax.shard_map(
         per_device,

time: 125 us -> 112 us (0.90)
  Pallas kernels: 122 us -> 108 us
  matrix products: 0 us -> 2.68 us
  local copies, waits for them, and re-layouts: 2.26 us -> 0 us
    pallas_call x1, Pallas kernels: 122 us -> 108 us  [per_device(): pl.pallas_call(functools.partial(kernel, n_row, n_col), out_shape=(jax.Sh...]
    dot_general x0 -> x1, matrix products: none -> 2.68 us  [dot(): return jnp.dot(left, right, preferred_element_type=F32)]
    unnamed x1 -> x0, local copies, waits for them, and re-layouts: 2.26 us -> none
where the time goes in v3:
time: 112 us; the launch traced here: 111 us
  Pallas kernels  108 us (96%)
  matrix products  2.68 us (2%)
    pallas_call x1, Pallas kernels, per_device(): pl.pallas_call(functools.partial(kernel, n_row, n_col), out_shape=(jax.Sh...  108 us
    dot_general x1, matrix products, dot(): return jnp.dot(left, right, preferred_element_type=F32)  2.68 us

profile of v3, /device:TPU:1, one launch (start us, length us, event | category | flops | bytes accessed | tf_op | source)
XLA Modules:
  0.0 111.0 jit_solution(9820284234486641344)
XLA Ops:
  0.0 108.4 %shard_map.73 = (f32[1024,256]{1,0:T(8,128)}, bf16[1024,160]{1,0:T(8,128)(2,1)}, bf16[160,256]{1,0:T(8,128)(2,1)}) custom-call(f32[1024,256]{1,0:T(8,128)} %bitcast.15, bf16[1536,1536]{1,0:T(8,128)(2,1)} %bitcast.13, bf16[1536,1536]{1,0:T(8,128)(2,1)} %bitcast.14, bf16[32,1536]{1,0:T(8,128)(2,1)} %bitcast.17, bf16[512,512]{1,0:T(8,128)(2,1)} %bitcast.16, ...), custom_call_target="tpu_custom_call" | custom-call | tf_op jit(solution)/shard_map/pallas_call | solution.py:464
  108.4 2.7 %fusion.1 = f32[1,1,1024,256]{3,2,1,0:T(8,128)} fusion(f32[1024,256]{1,0:T(8,128)} %get-tuple-element.8, bf16[1024,160]{1,0:T(8,128)(2,1)} %get-tuple-element.9, bf16[160,256]{1,0:T(8,128)(2,1)} %get-tuple-element.10), kind=kOutput, calls=%fused_computation.2 | convolution fusion | flops 84410368 | bytes 2506752 | tf_op jit(solution)/shard_map/dot_general | solution.py:33

commit v4 on v3

--- a/solution.py
+++ b/solution.py
@@ -55,9 +55,9 @@
 
 def kernel(
     n_row, n_col,
-    target_hbm, operator_hbm, inverse_hbm, basis_ref, coarse_hbm, rows_ref, counts_ref,
+    target_hbm, operator_hbm, inverse_hbm, basis_hbm, coarse_hbm, rows_hbm, counts_hbm,
     values_out, psi_out, around_ref,
-    operator, inverse, coarse, target, pick, spread, cross, ahead, total, image, values, held, first,
+    operator, inverse, coarse, target, basis_ref, rows_ref, counts_ref, pick, spread, cross, ahead, total, image, values, held, first,
     packed, ghosts, gather_src, gathered, part_src, parts, sums_src, sums, levels,
     basis_src, basis_tiles, wide_src, wide_tiles, assembled, psi, near_image, far_image,
     ghost_sums, near_sums, far_sums, own_sums,
@@ -102,11 +102,14 @@
                 (inverse_hbm, inverse),
                 (coarse_hbm, coarse),
                 (operator_hbm, operator),
+                (rows_hbm, rows_ref),
+                (counts_hbm, counts_ref),
+                (basis_hbm, basis_ref),
             )
         )
     ]
-    for load in loads:
-        load.start()
+    for i in (4, 5, 0, 6, 1, 2, 3):
+        loads[i].start()
 
     barrier = pltpu.get_barrier_semaphore()
     greeted = 0
@@ -249,8 +252,10 @@
     square = lax.broadcasted_iota(jnp.int32, (tile, tile), 0) == lax.broadcasted_iota(
         jnp.int32, (tile, tile), 1
     )
+    loads[4].wait()
+    loads[5].wait()
     lists = [
-        jnp.where(place < counts_ref[0, d], rows_ref[d : d + 1, :], -1).astype(F32)
+        jnp.where(place < counts_ref[:, d : d + 1], rows_ref[d : d + 1, :], -1).astype(F32)
         for d in range(tiles)
     ]
     along = lax.broadcasted_iota(jnp.int32, (tile, own), 1).astype(F32)
@@ -259,6 +264,8 @@
             jnp.where(square, jnp.broadcast_to(lists[d], (tile, tile)), 0.0), axis=1, keepdims=True
         )
         pick[d * tile : (d + 1) * tile, :] = jnp.where(along == upright, 1.0, 0.0).astype(HALF)
+    loads[6].wait()
+    for d in range(tiles):
         basis_src[d] = basis_ref[:, own + d * tile : own + (d + 1) * tile]
     loads[0].wait()
     held[...] = target[...].astype(HALF)
@@ -319,9 +326,9 @@
             assembled[k * level : (k + 1) * level, own + d * tile : own + (d + 1) * tile] = (
                 wide_tiles[d, e * level : (e + 1) * level, :]
             )
+    solve_rest(0, True)
     near_image[...] = dot_turned(operator[...], assembled[:near, :]).astype(HALF)
     far_image[...] = dot_turned(operator[:, own:], assembled[near:, own:]).astype(HALF)
-    solve_rest(0, True)
     ghost_sums[:near, :] = dot(assembled[:near, :], operator[:, own:]).astype(HALF)
     ghost_sums[near:, :] = dot(assembled[near:, own:], operator[own:, own:]).astype(HALF)
     near_sums[:near, :] = dot(assembled[:near, :], near_image[...]).astype(HALF)
@@ -341,23 +348,20 @@
     def sweep_once(sweep, carry):
         before = sweep - 1
         goes_on = sweep < ITERS - 1
-        margin = take_tiles(0, before)
-        image[own:, :] += dot(operator[own:, own:], margin)
-        own_sums[...] += dot(ghost_sums[...], margin)
         for k in range(NEAR, len(STENCIL)):
             level_copy(before, k).wait_recv()
         around = take_near(before)
         beyond = levels[before, NEAR:].reshape(-1, width)
-        owed = own_sums[...] + DAMPING * (dot(near_sums[...], around) + dot(far_sums[...], beyond))
+        own_sums[...] += DAMPING * (dot(near_sums[...], around) + dot(far_sums[...], beyond))
+        image[own:, :] += DAMPING * (
+            dot(near_image[own:, :], around) + dot(far_image[own:, :], beyond)
+        )
+        margin = take_tiles(0, before)
+        owed = own_sums[...] + dot(ghost_sums[...], margin)
         sums_src[sweep] = owed.astype(HALF).reshape(len(STENCIL), level, width)
         for k in OUTER_FIRST:
             sum_copy(sweep, k).start()
-        send_tiles(
-            1,
-            sweep,
-            image[own:, :]
-            + DAMPING * (dot(near_image[own:, :], around) + dot(far_image[own:, :], beyond)),
-        )
+        send_tiles(1, sweep, image[own:, :] + dot(operator[own:, own:], margin))
         image[:own, :] += dot(operator[:own, own:], margin) + DAMPING * (
             dot(near_image[:own, :], around) + dot(far_image[:own, :], beyond)
         )
@@ -440,6 +444,10 @@
         return carry
 
     lax.fori_loop(0, ITERS, settle, 0)
+
+
+def finish(values_ref, psi_ref, around_ref, out_ref):
+    out_ref[...] = values_ref[...] + DAMPING * dot(psi_ref[...], around_ref[...])
 
 
 def solution(mesh):
@@ -469,8 +477,7 @@
                 jax.ShapeDtypeStruct((near, width), HALF),
             ),
             in_specs=[
-                anywhere, anywhere, anywhere, vmem, anywhere, vmem,
-                pl.BlockSpec(memory_space=pltpu.SMEM),
+                anywhere, anywhere, anywhere, anywhere, anywhere, anywhere, anywhere,
             ],
             out_specs=(anywhere, anywhere, vmem),
             scratch_shapes=[
@@ -478,6 +485,9 @@
                 pltpu.VMEM((local, local), HALF),
                 pltpu.VMEM(coarse.shape, HALF),
                 pltpu.VMEM((own, width), F32),
+                pltpu.VMEM((level, local), HALF),
+                pltpu.VMEM((tiles, tile), jnp.int32),
+                pltpu.VMEM((1, tiles), jnp.int32),
                 pltpu.VMEM((rim, own), HALF),
                 pltpu.VMEM((own, rim), HALF),
                 pltpu.VMEM((rim, rim), HALF),
@@ -508,7 +518,7 @@
                 pltpu.VMEM((near + far, near), HALF),
                 pltpu.VMEM((near + far, far), HALF),
                 pltpu.VMEM((near + far, width), F32),
-                dma((4,)),
+                dma((7,)),
                 dma((2,)),
                 dma((4, ITERS, tiles)),
                 dma((4, ITERS, tiles)),
@@ -535,7 +545,19 @@
             rows_list,
             send_count[0],
         )
-        return (values + DAMPING * dot(psi, around))[None, None]
+        rows = own // 2
+        out = pl.pallas_call(
+            finish,
+            grid=(2,),
+            out_shape=jax.ShapeDtypeStruct((own, width), F32),
+            in_specs=[
+                pl.BlockSpec((rows, width), lambda i: (i, 0)),
+                pl.BlockSpec((rows, near), lambda i: (i, 0)),
+                pl.BlockSpec((near, width), lambda i: (0, 0)),
+            ],
+            out_specs=pl.BlockSpec((rows, width), lambda i: (i, 0)),
+        )(values, psi, around)
+        return out[None, None]
 
     return jax.shard_map(
         per_device,

time: 112 us -> 111 us (level)
  Pallas kernels: 108 us -> 111 us
  matrix products: 2.68 us -> 0 us
    dot_general x1 -> x0, matrix products: 2.68 us -> none  [dot(): return jnp.dot(left, right, preferred_element_type=F32)]
    pallas_call x0 -> x1, Pallas kernels: none -> 2.4 us  [per_device(): pl.pallas_call(finish, grid=(2,), out_shape=jax.ShapeDtypeStruct((own, wi...]
where the time goes in v4:
time: 111 us
  Pallas kernels  111 us (100%)
    pallas_call x1, Pallas kernels, per_device(): pl.pallas_call(functools.partial(kernel, n_row, n_col), out_shape=(jax.Sh...  108 us
    pallas_call x1, Pallas kernels, per_device(): pl.pallas_call(finish, grid=(2,), out_shape=jax.ShapeDtypeStruct((own, wi...  2.4 us

profile of v4, /device:TPU:1, one launch (start us, length us, event | category | flops | bytes accessed | tf_op | source)
XLA Modules:
  0.0 110.7 jit_solution(4340721438660062500)
XLA Ops:
  0.0 108.3 %shard_map.73 = (f32[1024,256]{1,0:T(8,128)}, bf16[1024,160]{1,0:T(8,128)(2,1)}, bf16[160,256]{1,0:T(8,128)(2,1)}) custom-call(f32[1024,256]{1,0:T(8,128)} %bitcast.12, bf16[1536,1536]{1,0:T(8,128)(2,1)} %bitcast.10, bf16[1536,1536]{1,0:T(8,128)(2,1)} %bitcast.11, bf16[32,1536]{1,0:T(8,128)(2,1)} %bitcast.14, bf16[512,512]{1,0:T(8,128)(2,1)} %bitcast.13, ...), custom_call_target="tpu_custom_call" | custom-call | tf_op jit(solution)/shard_map/pallas_call | solution.py:472
  108.3 2.4 %shard_map.74 = f32[1024,256]{1,0:T(8,128)} custom-call(f32[1024,256]{1,0:T(8,128)} %get-tuple-element.8.values_ref, bf16[1024,160]{1,0:T(8,128)(2,1)} %get-tuple-element.9.psi_ref, bf16[160,256]{1,0:T(8,128)(2,1)} %get-tuple-element.10.around_ref), custom_call_target="tpu_custom_call" | custom-call | tf_op jit(solution)/shard_map/pallas_call | solution.py:549

commit v5 on v4

--- a/solution.py
+++ b/solution.py
@@ -18,7 +18,7 @@
     (-2, 0), (2, 0), (-1, -1), (-1, 1), (1, -1), (1, 1), (0, -2), (0, 2),
 )
 NEAR = 5
-OUTER_FIRST = tuple(range(NEAR, len(STENCIL))) + tuple(range(1, NEAR))
+OUTER_FIRST = (7, 8, 9, 10, 5, 6, 1, 2, 11, 12, 3, 4)
 
 
 def stencil_index(down, right):
@@ -229,7 +229,7 @@
         levels[sweep, 0] = jnp.sum(parts[sweep].astype(F32), axis=0).astype(HALF)
 
         def outer():
-            for k in range(NEAR, len(STENCIL)):
+            for k in (7, 8, 9, 10, 5, 6, 11, 12):
                 level_copy(sweep, k).start()
 
         if far is True:

time: 111 us -> 109 us (0.982)
  Pallas kernels: 111 us -> 109 us
    pallas_call x1, Pallas kernels: 108 us -> 106 us  [per_device(): pl.pallas_call(functools.partial(kernel, n_row, n_col), out_shape=(jax.Sh...]
where the time goes in v5:
time: 109 us
  Pallas kernels  109 us (100%)
    pallas_call x1, Pallas kernels, per_device(): pl.pallas_call(functools.partial(kernel, n_row, n_col), out_shape=(jax.Sh...  106 us
    pallas_call x1, Pallas kernels, per_device(): pl.pallas_call(finish, grid=(2,), out_shape=jax.ShapeDtypeStruct((own, wi...  2.4 us

profile of v5, /device:TPU:1, one launch (start us, length us, event | category | flops | bytes accessed | tf_op | source)
XLA Modules:
  0.0 108.8 jit_solution(13615399811860423711)
XLA Ops:
  0.0 106.4 %shard_map.73 = (f32[1024,256]{1,0:T(8,128)}, bf16[1024,160]{1,0:T(8,128)(2,1)}, bf16[160,256]{1,0:T(8,128)(2,1)}) custom-call(f32[1024,256]{1,0:T(8,128)} %bitcast.12, bf16[1536,1536]{1,0:T(8,128)(2,1)} %bitcast.10, bf16[1536,1536]{1,0:T(8,128)(2,1)} %bitcast.11, bf16[32,1536]{1,0:T(8,128)(2,1)} %bitcast.14, bf16[512,512]{1,0:T(8,128)(2,1)} %bitcast.13, ...), custom_call_target="tpu_custom_call" | custom-call | tf_op jit(solution)/shard_map/pallas_call | solution.py:472
  106.4 2.4 %shard_map.74 = f32[1024,256]{1,0:T(8,128)} custom-call(f32[1024,256]{1,0:T(8,128)} %get-tuple-element.8.values_ref, bf16[1024,160]{1,0:T(8,128)(2,1)} %get-tuple-element.9.psi_ref, bf16[160,256]{1,0:T(8,128)(2,1)} %get-tuple-element.10.around_ref), custom_call_target="tpu_custom_call" | custom-call | tf_op jit(solution)/shard_map/pallas_call | solution.py:549
